TPU v7x, 256 devices: a whole 4x4x8 slice. The times are simulated.
256 devices in a mesh: section: 16 (over z_lo, y), tensor: 16 (over x, z_hi, core).
Axes of the slice: x: 4, y: 4, z: 8 (z_hi: 2, z_lo: 4; z = z_hi * 4 + z_lo), core: 2. Of those that a mesh axis runs over, the one named last changes fastest.
Arguments:
- inputs_down: bfloat16 [16, 224, 8192], P('section', None, 'tensor'), may hold values from -18 to 18
- inputs_up: bfloat16 [16, 224, 8192], P('section', None, 'tensor'), may hold values from -18 to 18
- grads_down: bfloat16 [16, 224, 8192], P('section', None, 'tensor'), may hold values from -6 to 6
- grads_up: bfloat16 [16, 224, 8192], P('section', None, 'tensor'), may hold values from -6 to 6
- weights_down: bfloat16 [16, 8192, 2048], P('section', 'tensor'), may hold values from -0.5 to 0.5
- weights_up: bfloat16 [16, 8192, 2048], P('section', 'tensor'), may hold values from -0.5 to 0.5
Outputs:
- handed_down: bfloat16 [16, 224, 8192], P('section', None, 'tensor')
- handed_up: bfloat16 [16, 224, 8192], P('section', None, 'tensor')
- returned_down: bfloat16 [16, 224, 8192], P('section', None, 'tensor')
- returned_up: bfloat16 [16, 224, 8192], P('section', None, 'tensor')
- weight_grads: float32 [16, 8192, 2048], P('section', 'tensor')
All inputs are finite; a program needn't handle non-finite values.
Results may differ from a plain program's by a relative error of at most 0.0095.
Values may be sent and summed in bfloat16 or wider, within the bound.
A program may use at most 64 MiB of HBM per device.

v0:
```python
import jax
import jax.numpy as jnp
from jax import lax
from jax.sharding import PartitionSpec as P

D = 8192
HEADS = 64
KV_HEADS = 8
HEAD_DIM = 128
EPS = 1e-05
NEG_BIG = -1e30


def cut_along(x, dim, count):
    before, after = (x.shape[:dim], x.shape[dim + 1 :])
    return jnp.moveaxis(x.reshape(*before, count, -1, *after), dim, 0)


def sum_at_owner(x, axis, dim):
    count = lax.axis_size(axis)
    tiles = lax.all_to_all(cut_along(x, dim, count), axis, 0, 0, tiled=True)
    return jnp.sum(tiles, axis=0)


def shortened(x):

    def short(part):
        return part.astype(jnp.bfloat16) if part.dtype == jnp.float32 else part

    return jax.tree.map(short, x)


def copy_for_each(x, axis):
    count = lax.axis_size(axis)
    return lax.all_to_all(jnp.broadcast_to(x[None], (count, *x.shape)), axis, 0, 0, tiled=True)


def taken_together(x, axis):
    return copy_for_each(x, axis).sum(axis=0)


def passed_along(x, axis, by):
    count = lax.axis_size(axis)
    pairs = [(i, i + by) for i in range(count) if 0 <= i + by < count]
    return lax.ppermute(x, axis, pairs)


def combine_tensor(partial_value):
    share = sum_at_owner(partial_value, "tensor", 1).astype(jnp.bfloat16)
    return lax.all_gather(share, "tensor", axis=1, tiled=True)


def reflect_blocks(parts):
    flipped = tuple((jnp.flip(piece, 1) for piece in parts))
    return jax.tree.map(
        lambda part, own: part.astype(own.dtype),
        lax.all_to_all(shortened(flipped), "section", split_axis=1, concat_axis=1, tiled=True),
        flipped,
    )


def mirror_terms(payload):
    sections = lax.axis_size("section")
    split = tuple(
        (piece.reshape(piece.shape[0], sections, piece.shape[1] // sections) for piece in payload)
    )
    moved = reflect_blocks(
        (
            lax.all_to_all(split[0], "section", split_axis=1, concat_axis=1, tiled=True),
            lax.all_to_all(split[1], "section", split_axis=1, concat_axis=1, tiled=True),
        )
    )
    return tuple(
        (piece.reshape(piece.shape[0], piece.shape[1] * piece.shape[2]) for piece in moved)
    )


def section_pass(inputs, grads, weights):
    tokens, width_here = inputs.shape
    heads_here = width_here // HEAD_DIM
    kv_width = weights.shape[1] // 2
    scale = HEAD_DIM ** (-0.5)
    x_float = inputs.astype(jnp.float32)
    squares = taken_together(jnp.sum(x_float * x_float, axis=1), "tensor")
    scale_rows = lax.rsqrt(squares / D + EPS)[:, None]
    normed = x_float * scale_rows
    hidden = normed.astype(jnp.bfloat16)
    keyval = combine_tensor(jnp.dot(hidden, weights, preferred_element_type=jnp.float32))
    head_ids = lax.axis_index("tensor") * heads_here + jnp.arange(heads_here)
    selector = (head_ids[:, None] // (HEADS // KV_HEADS) == jnp.arange(KV_HEADS)[None, :]).astype(
        jnp.float32
    )
    keys_all = keyval[:, :kv_width].reshape(tokens, KV_HEADS, HEAD_DIM).astype(jnp.float32)
    values_all = keyval[:, kv_width:].reshape(tokens, KV_HEADS, HEAD_DIM).astype(jnp.float32)
    key_rows = jnp.einsum("hj,ljd->lhd", selector, keys_all)
    value_rows = jnp.einsum("hj,ljd->lhd", selector, values_all)
    queries = hidden.reshape(tokens, heads_here, HEAD_DIM).astype(jnp.float32)
    places = jnp.arange(tokens)
    causal = places[:, None] >= places[None, :]
    scores = jnp.einsum("qhd,khd->hqk", queries, key_rows) * scale
    scores = jnp.where(causal[None], scores, NEG_BIG)
    score_peak = jnp.max(scores, axis=-1, keepdims=True)
    score_exp = jnp.exp(scores - score_peak)
    attn_probs = score_exp / jnp.sum(score_exp, axis=-1, keepdims=True)
    probs_low = lax.optimization_barrier(attn_probs.astype(jnp.bfloat16)).astype(jnp.float32)
    attended = jnp.einsum("hqk,khd->qhd", probs_low, value_rows).reshape(tokens, width_here)
    output = (x_float + attended).astype(jnp.bfloat16)
    upstream = grads.astype(jnp.float32).reshape(tokens, heads_here, HEAD_DIM)
    grad_prob = jnp.einsum("qhd,khd->hqk", upstream, value_rows)
    grad_value_heads = jnp.einsum("hqk,qhd->khd", probs_low, upstream)
    grad_score = attn_probs * (grad_prob - jnp.sum(attn_probs * grad_prob, axis=-1, keepdims=True))
    grad_score_low = lax.optimization_barrier(grad_score.astype(jnp.bfloat16)).astype(jnp.float32)
    grad_query = jnp.einsum("hqk,khd->qhd", grad_score_low, key_rows) * scale
    grad_key_heads = jnp.einsum("hqk,qhd->khd", grad_score_low, queries) * scale
    grad_keys = jnp.einsum("hj,lhd->ljd", selector, grad_key_heads).reshape(tokens, kv_width)
    grad_values = jnp.einsum("hj,lhd->ljd", selector, grad_value_heads).reshape(tokens, kv_width)
    grad_kv = combine_tensor(jnp.concatenate([grad_keys, grad_values], axis=1))
    grad_hidden = grad_query.reshape(tokens, width_here) + jnp.dot(
        grad_kv, weights.T, preferred_element_type=jnp.float32
    )
    inner_sum = taken_together(jnp.sum(grad_hidden * normed, axis=1), "tensor")
    grad_input = (
        grads.astype(jnp.float32) + scale_rows * (grad_hidden - normed * (inner_sum / D)[:, None])
    ).astype(jnp.bfloat16)
    grad_weights = jnp.dot(hidden.T, grad_kv, preferred_element_type=jnp.float32)
    return (output, grad_input, grad_weights, hidden, grad_kv)


def on_device(inputs_down, inputs_up, grads_down, grads_up, weights_down, weights_up):
    out_down, back_down, dw_down, hidden_down, gkv_down = section_pass(
        inputs_down[0], grads_down[0], weights_down[0]
    )
    handed_down = passed_along(out_down, "section", 1)
    out_up, back_up, dw_up, hidden_up, gkv_up = section_pass(
        inputs_up[0], grads_up[0], weights_up[0]
    )
    handed_up = passed_along(out_up, "section", -1)
    returned_down = passed_along(back_down, "section", -1)
    returned_up = passed_along(back_up, "section", 1)
    carried_hidden, carried_kv = mirror_terms((hidden_up, gkv_up))
    weight_grads = dw_down + jnp.dot(
        carried_hidden.T, carried_kv, preferred_element_type=jnp.float32
    )
    return (
        handed_down[None],
        handed_up[None],
        returned_down[None],
        returned_up[None],
        weight_grads[None],
    )


def solution(mesh):
    in_specs = (
        P("section", None, "tensor"),
        P("section", None, "tensor"),
        P("section", None, "tensor"),
        P("section", None, "tensor"),
        P("section", "tensor", None),
        P("section", "tensor", None),
    )
    out_specs = (
        P("section", None, "tensor"),
        P("section", None, "tensor"),
        P("section", None, "tensor"),
        P("section", None, "tensor"),
        P("section", "tensor", None),
    )
    return jax.shard_map(
        on_device, mesh=mesh, in_specs=in_specs, out_specs=out_specs, check_vma=False
    )
```

profile of v0, /device:TPU:64, one launch (start us, length us, event | category | flops | bytes accessed | tf_op | source)
XLA Modules:
  0.0 522.0 jit_solution(3485464926994449465)
XLA Ops:
  2.5 9.2 %all-to-all-start.2 = ((f32[16,1,224]{2,1,0:T(1,128)}), f32[16,1,224]{2,1,0:T(1,128)S(1)}, u32[]{:S(2)}, u32[]{:S(2)}) async-start(f32[16,1,224]{2,1,0:T(1,128)} %broadcast_in_dim.40), calls=%async_computation.2 | async-start | bytes 32768 | tf_op jit(solution)/shard_map/all_to_all | solution.py:35
  13.9 7.8 %all-to-all-done.2 = f32[16,1,224]{2,1,0:T(1,128)S(1)} async-done(((f32[16,1,224]{2,1,0:T(1,128)}), f32[16,1,224]{2,1,0:T(1,128)S(1)}, u32[]{:S(2)}, u32[]{:S(2)}) %all-to-all-start.2) | async-done | bytes 14368 | tf_op jit(solution)/shard_map/all_to_all | solution.py:35
  22.3 3.5 all-to-all-start
  26.6 9.1 %all-to-all-done = f32[16,1,224]{2,1,0:T(1,128)S(1)} async-done(((f32[16,1,224]{2,1,0:T(1,128)}), f32[16,1,224]{2,1,0:T(1,128)S(1)}, u32[]{:S(2)}, u32[]{:S(2)}) %all-to-all-start) | async-done | bytes 14368 | tf_op jit(solution)/shard_map/all_to_all | solution.py:35
  35.8 7.3 %all-to-all-start.8 = ((bf16[224,16,32]{0,2,1:T(8,128)(2,1)}), bf16[224,16,32]{0,2,1:T(8,128)(2,1)S(1)}, u32[]{:S(2)}, u32[]{:S(2)}) async-start(bf16[224,16,32]{0,2,1:T(8,128)(2,1)} %multiply_convert_fusion), calls=%async_computation.8 | async-start | bytes 524288 | tf_op jit(solution)/shard_map/all_to_all | solution.py:69
  45.6 3.6 convolution_bitcast_fusion
  49.2 3.0 all-to-all-done.8
  52.2 4.4 all-to-all-start.3
  56.7 4.0 copy.194
  60.7 3.6 convolution_bitcast_fusion.1
  64.3 40.8 %all-to-all-done.3 = f32[16,224,128]{2,1,0:T(8,128)} async-done(((f32[16,224,128]{2,1,0:T(8,128)}), f32[16,224,128]{2,1,0:T(8,128)}, u32[]{:S(2)}, u32[]{:S(2)}) %all-to-all-start.3) | async-done | bytes 1835040 | tf_op jit(solution)/shard_map/all_to_all | solution.py:21
  105.1 4.4 all-to-all-start.1
  114.8 60.1 %all_gather.13 = bf16[224,2048]{1,0:T(8,128)(2,1)S(1)} all-gather(bf16[224,128]{1,0:T(8,128)(2,1)S(1)} %reduce_sum.150), channel_id=1, replica_groups=mesh['section'=16,'tensor'=16] {'tensor'}, dimensions={1}, use_global_device_ids=true | all-gather | bytes 974848 | tf_op jit(solution)/shard_map/all_gather | solution.py:50
  184.2 13.6 %all-to-all-start.9 = ((bf16[224,16,32]{0,2,1:T(8,128)(2,1)}), bf16[224,16,32]{0,2,1:T(8,128)(2,1)S(1)}, u32[]{:S(2)}, u32[]{:S(2)}) async-start(bf16[224,16,32]{0,2,1:T(8,128)(2,1)} %rev.8), calls=%async_computation.9 | async-start | bytes 524288 | tf_op jit(solution)/shard_map/all_to_all | solution.py:57
  203.1 4.2 all-to-all-done.9
  207.2 8.9 %all-to-all-start.6 = ((f32[16,224,128]{2,1,0:T(8,128)}), f32[16,224,128]{2,1,0:T(8,128)}, u32[]{:S(2)}, u32[]{:S(2)}) async-start(f32[16,224,128]{2,1,0:T(8,128)} %copy.185), calls=%async_computation.6 | async-start | bytes 3670016 | tf_op jit(solution)/shard_map/all_to_all | solution.py:21
  216.1 72.7 %all_gather.12 = bf16[224,2048]{1,0:T(8,128)(2,1)S(1)} all-gather(bf16[224,128]{1,0:T(8,128)(2,1)S(1)} %reduce_sum.146), channel_id=1, replica_groups=mesh['section'=16,'tensor'=16] {'tensor'}, dimensions={1}, use_global_device_ids=true | all-gather | bytes 974848 | tf_op jit(solution)/shard_map/all_gather | solution.py:50
  298.9 9.7 %all-to-all-start.4 = ((f32[16,224,128]{2,1,0:T(8,128)}), f32[16,224,128]{2,1,0:T(8,128)}, u32[]{:S(2)}, u32[]{:S(2)}) async-start(f32[16,224,128]{2,1,0:T(8,128)} %copy.175), calls=%async_computation.4 | async-start | bytes 3670016 | tf_op jit(solution)/shard_map/all_to_all | solution.py:21
  311.3 71.0 %all_gather.15 = bf16[224,2048]{1,0:T(8,128)(2,1)S(1)} all-gather(bf16[224,128]{1,0:T(8,128)(2,1)S(1)} %reduce_sum.157), channel_id=1, replica_groups=mesh['section'=16,'tensor'=16] {'tensor'}, dimensions={1}, use_global_device_ids=true | all-gather | bytes 974848 | tf_op jit(solution)/shard_map/all_gather | solution.py:50
  385.5 8.5 %all-to-all-start.7 = ((f32[16,1,224]{2,1,0:T(1,128)}), f32[16,1,224]{2,1,0:T(1,128)S(1)}, u32[]{:S(2)}, u32[]{:S(2)}) async-start(f32[16,1,224]{2,1,0:T(1,128)} %broadcast_in_dim.44), calls=%async_computation.7 | async-start | bytes 32768 | tf_op jit(solution)/shard_map/all_to_all | solution.py:35
  395.2 8.9 %all-to-all-done.7 = f32[16,1,224]{2,1,0:T(1,128)S(1)} async-done(((f32[16,1,224]{2,1,0:T(1,128)}), f32[16,1,224]{2,1,0:T(1,128)S(1)}, u32[]{:S(2)}, u32[]{:S(2)}) %all-to-all-start.7) | async-done | bytes 14368 | tf_op jit(solution)/shard_map/all_to_all | solution.py:35
  404.1 4.4 all-to-all-start.10
  412.5 36.8 %all_gather.14 = bf16[224,2048]{1,0:T(8,128)(2,1)S(1)} all-gather(bf16[224,128]{1,0:T(8,128)(2,1)S(1)} %reduce_sum.153), channel_id=1, replica_groups=mesh['section'=16,'tensor'=16] {'tensor'}, dimensions={1}, use_global_device_ids=true | all-gather | bytes 974848 | tf_op jit(solution)/shard_map/all_gather | solution.py:50
  452.6 8.0 %all-to-all-start.5 = ((f32[16,1,224]{2,1,0:T(1,128)}), f32[16,1,224]{2,1,0:T(1,128)S(1)}, u32[]{:S(2)}, u32[]{:S(2)}) async-start(f32[16,1,224]{2,1,0:T(1,128)} %broadcast_in_dim.42), calls=%async_computation.5 | async-start | bytes 32768 | tf_op jit(solution)/shard_map/all_to_all | solution.py:35
  462.8 7.7 %all-to-all-done.5 = f32[16,1,224]{2,1,0:T(1,128)S(1)} async-done(((f32[16,1,224]{2,1,0:T(1,128)}), f32[16,1,224]{2,1,0:T(1,128)S(1)}, u32[]{:S(2)}, u32[]{:S(2)}) %all-to-all-start.5) | async-done | bytes 14368 | tf_op jit(solution)/shard_map/all_to_all | solution.py:35
  470.6 9.9 %all-to-all-start.11 = ((bf16[224,16,128]{2,0,1:T(8,128)(2,1)}), bf16[224,16,128]{2,0,1:T(8,128)(2,1)S(1)}, u32[]{:S(2)}, u32[]{:S(2)}) async-start(bf16[224,16,128]{2,0,1:T(8,128)(2,1)} %rev.9), calls=%async_computation.11 | async-start | bytes 1835008 | tf_op jit(solution)/shard_map/all_to_all | solution.py:57
  485.3 3.4 collective-permute-start.3
  488.6 4.6 collective-permute-start.1
  496.0 3.5 collective-permute-start
  502.3 6.8 %collective-permute-done.3 = bf16[224,512]{1,0:T(8,128)(2,1)S(1)} collective-permute-done((bf16[224,512]{1,0:T(8,128)(2,1)}, bf16[224,512]{1,0:T(8,128)(2,1)S(1)}, u32[]{:S(2)}, u32[]{:S(2)}) %collective-permute-start.3) | collective-permute-done | bytes 229408 | tf_op jit(solution)/shard_map/ppermute | solution.py:45
  510.1 3.2 collective-permute-done
  513.4 4.9 add_bitcast_fusion
  (135 shorter events, 69.3 us)
Async XLA Ops:
  0.6 42.4 %copy-start.1 = (bf16[1,512,2048]{2,1,0:T(8,128)(2,1)S(1)}, bf16[1,512,2048]{2,1,0:T(8,128)(2,1)}, u32[]{:S(2)}) copy-start(bf16[1,512,2048]{2,1,0:T(8,128)(2,1)} %param.11) | copy-start | bytes 6291460
  2.5 19.2 %all-to-all-start.2 = ((f32[16,1,224]{2,1,0:T(1,128)}), f32[16,1,224]{2,1,0:T(1,128)S(1)}, u32[]{:S(2)}, u32[]{:S(2)}) async-start(f32[16,1,224]{2,1,0:T(1,128)} %broadcast_in_dim.40), calls=%async_computation.2 | async-start | bytes 32768 | tf_op jit(solution)/shard_map/all_to_all | solution.py:35
  22.3 13.4 %all-to-all-start = ((f32[16,1,224]{2,1,0:T(1,128)}), f32[16,1,224]{2,1,0:T(1,128)S(1)}, u32[]{:S(2)}, u32[]{:S(2)}) async-start(f32[16,1,224]{2,1,0:T(1,128)} %broadcast_in_dim.36), calls=%async_computation | async-start | bytes 32768 | tf_op jit(solution)/shard_map/all_to_all | solution.py:35
  35.8 16.5 %all-to-all-start.8 = ((bf16[224,16,32]{0,2,1:T(8,128)(2,1)}), bf16[224,16,32]{0,2,1:T(8,128)(2,1)S(1)}, u32[]{:S(2)}, u32[]{:S(2)}) async-start(bf16[224,16,32]{0,2,1:T(8,128)(2,1)} %multiply_convert_fusion), calls=%async_computation.8 | async-start | bytes 524288 | tf_op jit(solution)/shard_map/all_to_all | solution.py:69
  52.2 52.9 %all-to-all-start.3 = ((f32[16,224,128]{2,1,0:T(8,128)}), f32[16,224,128]{2,1,0:T(8,128)}, u32[]{:S(2)}, u32[]{:S(2)}) async-start(f32[16,224,128]{2,1,0:T(8,128)} %convolution_bitcast_fusion), calls=%async_computation.3 | async-start | bytes 3670016 | tf_op jit(solution)/shard_map/all_to_all | solution.py:21
  56.7 4.0 copy-start
  64.3 47.1 %copy-start.22 = (bf16[1,224,512]{2,1,0:T(8,128)(2,1)S(1)}, bf16[1,224,512]{2,1,0:T(8,128)(2,1)}, u32[]{:S(2)}) copy-start(bf16[1,224,512]{2,1,0:T(8,128)(2,1)} %param.8) | copy-start | bytes 688132
  105.1 79.1 %all-to-all-start.1 = ((f32[16,224,128]{2,1,0:T(8,128)}), f32[16,224,128]{2,1,0:T(8,128)}, u32[]{:S(2)}, u32[]{:S(2)}) async-start(f32[16,224,128]{2,1,0:T(8,128)} %convolution_bitcast_fusion.1), calls=%async_computation.1 | async-start | bytes 3670016 | tf_op jit(solution)/shard_map/all_to_all | solution.py:21
  176.2 3.9 copy-start.24
  184.2 23.0 %all-to-all-start.9 = ((bf16[224,16,32]{0,2,1:T(8,128)(2,1)}), bf16[224,16,32]{0,2,1:T(8,128)(2,1)S(1)}, u32[]{:S(2)}, u32[]{:S(2)}) async-start(bf16[224,16,32]{0,2,1:T(8,128)(2,1)} %rev.8), calls=%async_computation.9 | async-start | bytes 524288 | tf_op jit(solution)/shard_map/all_to_all | solution.py:57
  207.2 8.9 %copy-start.18 = (bf16[224,16,32]{0,2,1:T(8,128)(2,1)}, bf16[224,16,32]{0,2,1:T(8,128)(2,1)S(1)}, u32[]{:S(2)}) copy-start(bf16[224,16,32]{0,2,1:T(8,128)(2,1)S(1)} %all-to-all-done.9) | copy-start | bytes 688132
  207.2 91.7 %all-to-all-start.6 = ((f32[16,224,128]{2,1,0:T(8,128)}), f32[16,224,128]{2,1,0:T(8,128)}, u32[]{:S(2)}, u32[]{:S(2)}) async-start(f32[16,224,128]{2,1,0:T(8,128)} %copy.185), calls=%async_computation.6 | async-start | bytes 3670016 | tf_op jit(solution)/shard_map/all_to_all | solution.py:21
  289.8 4.3 copy-start.14
  290.2 3.9 copy-start.26
  298.9 9.7 %copy-start.12 = (bf16[4,224,224]{1,2,0:T(8,128)(2,1)S(1)}, bf16[4,224,224]{1,2,0:T(8,128)(2,1)}, u32[]{:S(2)}) copy-start(bf16[4,224,224]{1,2,0:T(8,128)(2,1)} %copy-done.11) | copy-start | bytes 1204228
  298.9 9.7 %copy-start.25 = (bf16[224,4,128]{2,1,0:T(4,128)(2,1)S(1)}, bf16[224,4,128]{2,1,0:T(4,128)(2,1)}, u32[]{:S(2)}) copy-start(bf16[224,4,128]{2,1,0:T(4,128)(2,1)} %copy-done.24) | copy-start | bytes 688132
  298.9 86.0 %all-to-all-start.4 = ((f32[16,224,128]{2,1,0:T(8,128)}), f32[16,224,128]{2,1,0:T(8,128)}, u32[]{:S(2)}, u32[]{:S(2)}) async-start(f32[16,224,128]{2,1,0:T(8,128)} %copy.175), calls=%async_computation.4 | async-start | bytes 3670016 | tf_op jit(solution)/shard_map/all_to_all | solution.py:21
  385.5 18.5 %all-to-all-start.7 = ((f32[16,1,224]{2,1,0:T(1,128)}), f32[16,1,224]{2,1,0:T(1,128)S(1)}, u32[]{:S(2)}, u32[]{:S(2)}) async-start(f32[16,1,224]{2,1,0:T(1,128)} %broadcast_in_dim.44), calls=%async_computation.7 | async-start | bytes 32768 | tf_op jit(solution)/shard_map/all_to_all | solution.py:35
  404.1 47.9 %all-to-all-start.10 = ((bf16[224,16,128]{2,0,1:T(8,128)(2,1)}), bf16[224,16,128]{2,0,1:T(8,128)(2,1)}, u32[]{:S(2)}, u32[]{:S(2)}) async-start(bf16[224,16,128]{2,0,1:T(8,128)(2,1)} %copy_bitcast_fusion), calls=%async_computation.10 | async-start | bytes 1835008 | tf_op jit(solution)/shard_map/all_to_all | solution.py:70
  408.5 40.8 %copy-start.2 = (bf16[1,512,2048]{2,1,0:T(8,128)(2,1)S(1)}, bf16[1,512,2048]{2,1,0:T(8,128)(2,1)}, u32[]{:S(2)}) copy-start(bf16[1,512,2048]{2,1,0:T(8,128)(2,1)} %param.10) | copy-start | bytes 6291460
  452.0 28.5 %copy-start.5 = (bf16[4,224,224]{1,2,0:T(8,128)(2,1)S(1)}, bf16[4,224,224]{1,2,0:T(8,128)(2,1)}, u32[]{:S(2)}) copy-start(bf16[4,224,224]{1,2,0:T(8,128)(2,1)} %copy-done.4) | copy-start | bytes 1204228
  452.0 28.5 %copy-start.9 = (bf16[224,4,128]{2,1,0:T(4,128)(2,1)S(1)}, bf16[224,4,128]{2,1,0:T(4,128)(2,1)}, u32[]{:S(2)}) copy-start(bf16[224,4,128]{2,1,0:T(4,128)(2,1)} %copy-done.8) | copy-start | bytes 688132
  452.6 18.0 %all-to-all-start.5 = ((f32[16,1,224]{2,1,0:T(1,128)}), f32[16,1,224]{2,1,0:T(1,128)S(1)}, u32[]{:S(2)}, u32[]{:S(2)}) async-start(f32[16,1,224]{2,1,0:T(1,128)} %broadcast_in_dim.42), calls=%async_computation.5 | async-start | bytes 32768 | tf_op jit(solution)/shard_map/all_to_all | solution.py:35
  460.6 21.0 %copy-start.7 = (bf16[4,224,224]{1,2,0:T(8,128)(2,1)S(1)}, bf16[4,224,224]{1,2,0:T(8,128)(2,1)}, u32[]{:S(2)}) copy-start(bf16[4,224,224]{1,2,0:T(8,128)(2,1)} %copy-done.6) | copy-start | bytes 1204228
  470.6 42.8 %all-to-all-start.11 = ((bf16[224,16,128]{2,0,1:T(8,128)(2,1)}), bf16[224,16,128]{2,0,1:T(8,128)(2,1)S(1)}, u32[]{:S(2)}, u32[]{:S(2)}) async-start(bf16[224,16,128]{2,0,1:T(8,128)(2,1)} %rev.9), calls=%async_computation.11 | async-start | bytes 1835008 | tf_op jit(solution)/shard_map/all_to_all | solution.py:57
  481.6 11.7 %copy-start.23 = (bf16[1,224,512]{2,1,0:T(8,128)(2,1)S(1)}, bf16[1,224,512]{2,1,0:T(8,128)(2,1)}, u32[]{:S(2)}) copy-start(bf16[1,224,512]{2,1,0:T(8,128)(2,1)} %param.8) | copy-start | bytes 688132
  482.9 10.3 %copy-start.17 = (f32[224,512]{1,0:T(8,128)S(1)}, f32[224,512]{1,0:T(8,128)}, u32[]{:S(2)}) copy-start(f32[224,512]{1,0:T(8,128)} %get-tuple-element.16) | copy-start | bytes 1376260
  485.3 23.9 %collective-permute-start.3 = (bf16[224,512]{1,0:T(8,128)(2,1)}, bf16[224,512]{1,0:T(8,128)(2,1)S(1)}, u32[]{:S(2)}, u32[]{:S(2)}) collective-permute-start(bf16[224,512]{1,0:T(8,128)(2,1)} %get-tuple-element.9), channel_id=1, source_target_pairs={{0,16},{16,32},{32,48},{48,64},{64,80},{80,96},{96,112},{112,128},... | collective-permute-start | bytes 688136 | tf_op jit(solution)/shard_map/ppermute | solution.py:45
  488.6 20.6 %collective-permute-start.1 = (bf16[224,512]{1,0:T(8,128)(2,1)}, bf16[224,512]{1,0:T(8,128)(2,1)}, u32[]{:S(2)}, u32[]{:S(2)}) collective-permute-start(bf16[224,512]{1,0:T(8,128)(2,1)} %get-tuple-element.10), channel_id=1, source_target_pairs={{16,0},{32,16},{48,32},{64,48},{80,64},{96,80},{112,96},{128,112},... | collective-permute-start | bytes 688136 | tf_op jit(solution)/shard_map/ppermute | solution.py:45
  493.5 16.6 %collective-permute-start.2 = (bf16[224,512]{1,0:T(8,128)(2,1)S(1)}, bf16[224,512]{1,0:T(8,128)(2,1)S(1)}, u32[]{:S(2)}, u32[]{:S(2)}) collective-permute-start(bf16[224,512]{1,0:T(8,128)(2,1)S(1)} %get-tuple-element.11), channel_id=1, source_target_pairs={{16,0},{32,16},{48,32},{64,48},{80,64},{96,80},{112,96},{128,112},... | collective-permute-start | bytes 688136 | tf_op jit(solution)/shard_map/ppermute | solution.py:45
  496.0 17.4 %copy-start.19 = (bf16[224,16,32]{0,2,1:T(8,128)(2,1)S(1)}, bf16[224,16,32]{0,2,1:T(8,128)(2,1)}, u32[]{:S(2)}) copy-start(bf16[224,16,32]{0,2,1:T(8,128)(2,1)} %copy-done.18) | copy-start | bytes 688132
  496.0 17.4 %collective-permute-start = (bf16[224,512]{1,0:T(8,128)(2,1)S(1)}, bf16[224,512]{1,0:T(8,128)(2,1)S(1)}, u32[]{:S(2)}, u32[]{:S(2)}) collective-permute-start(bf16[224,512]{1,0:T(8,128)(2,1)S(1)} %get-tuple-element.12), channel_id=1, source_target_pairs={{0,16},{16,32},{32,48},{48,64},{64,80},{80,96},{96,112},{112,128},... | collective-permute-start | bytes 688136 | tf_op jit(solution)/shard_map/ppermute | solution.py:45
  (11 other events, 17.0 us)
where the time goes:
time: 524 us; the launch traced here: 522 us
  blocking collectives  241 us (46%)
  starting transfers between devices  106 us (20%)
  waiting for transfers between devices  92.6 us (18%)
  matrix products  39 us (7%)
  local copies, waits for them, and re-layouts  27.4 us (5%)
  other arithmetic  15.6 us (3%)
    all_gather x4, blocking collectives, combine_tensor(): return lax.all_gather(share, 'tensor', axis=1, tiled=True)  241 us
    all_to_all x4, waiting for transfers between devices, sum_at_owner(): tiles = lax.all_to_all(cut_along(x, dim, count), axis, 0, 0, tiled=True)  40.8 us
    all_to_all x4, waiting for transfers between devices, copy_for_each(): lax.all_to_all(jnp.broadcast_to(x[None], (count, *x.shape)), axis, 0, 0,...  33.6 us
    all_to_all x4, starting transfers between devices, copy_for_each(): lax.all_to_all(jnp.broadcast_to(x[None], (count, *x.shape)), axis, 0, 0,...  29.2 us
    all_to_all x4, starting transfers between devices, sum_at_owner(): tiles = lax.all_to_all(cut_along(x, dim, count), axis, 0, 0, tiled=True)  27.4 us
    all_to_all x2, starting transfers between devices, reflect_blocks(): lax.all_to_all(shortened(flipped), 'section', split_axis=1, concat_axis=1...  23.5 us
    ppermute x4, starting transfers between devices, passed_along(): return lax.ppermute(x, axis, pairs)  13.9 us
    ppermute x4, waiting for transfers between devices, passed_along(): return lax.ppermute(x, axis, pairs)  11 us
  transfers between devices with their start and end apart: 16, of which 10 were waited for; matrix products, arithmetic and copies ran while one was open for 13% of the time, Pallas kernels for 0%

commit v1 on v0

--- a/solution.py
+++ b/solution.py
@@ -47,7 +47,9 @@
 
 def combine_tensor(partial_value):
     share = sum_at_owner(partial_value, "tensor", 1).astype(jnp.bfloat16)
-    return lax.all_gather(share, "tensor", axis=1, tiled=True)
+    return jnp.concatenate(
+        lax.all_to_all(jnp.stack([share] * lax.axis_size("tensor")), "tensor", 0, 0), axis=1
+    )
 
 
 def reflect_blocks(parts):

time: 524 us -> 490 us (0.935)
  blocking collectives: 241 us -> 13 us
  waiting for transfers between devices: 92.6 us -> 281 us
  matrix products: 39 us -> 32.6 us
  starting transfers between devices: 106 us -> 112 us
  local copies, waits for them, and re-layouts: 27.4 us -> 33.1 us
    all_gather x4 -> x0, blocking collectives: 241 us -> none  [combine_tensor(): return lax.all_gather(share, 'tensor', axis=1, tiled=True)]
    all_to_all x4, waiting for transfers between devices: 40.8 us -> 149 us  [sum_at_owner(): tiles = lax.all_to_all(cut_along(x, dim, count), axis, 0, 0, tiled=True)]
    all_to_all x0 -> x4, waiting for transfers between devices: none -> 67.9 us  [combine_tensor(): lax.all_to_all(jnp.stack([share] * lax.axis_size('tensor')), 'tensor', 0, 0)]
    all_to_all x0 -> x4, starting transfers between devices: none -> 18.9 us  [combine_tensor(): lax.all_to_all(jnp.stack([share] * lax.axis_size('tensor')), 'tensor', 0, 0)]
    all_to_all x1, waiting for transfers between devices: 0.01 us -> 18.7 us  [mirror_terms(): lax.all_to_all(split[1], 'section', split_axis=1, concat_axis=1, tiled=True)]
    all_to_all x1, starting transfers between devices: 4.43 us -> 21.1 us  [mirror_terms(): lax.all_to_all(split[1], 'section', split_axis=1, concat_axis=1, tiled=True)]
    all_to_all x4 -> x3, starting transfers between devices: 29.2 us -> 16.2 us  [copy_for_each(): lax.all_to_all(jnp.broadcast_to(x[None], (count, *x.shape)), axis, 0, 0,...]
    all_to_all x0 -> x1, blocking collectives: none -> 13 us  [copy_for_each(): lax.all_to_all(jnp.broadcast_to(x[None], (count, *x.shape)), axis, 0, 0,...]
  transfers between devices with their start and end apart: 16 -> 19, of which waited for: 10 -> 17; matrix products, arithmetic and copies ran while one was open for 13% -> 13% of each run, Pallas kernels for 0% -> 0%
where the time goes in v1:
time: 490 us; the launch traced here: 487 us
  waiting for transfers between devices  281 us (57%)
  starting transfers between devices  112 us (23%)
  local copies, waits for them, and re-layouts  33.1 us (7%)
  matrix products  32.6 us (7%)
  other arithmetic  14.5 us (3%)
  blocking collectives  13 us (3%)
    all_to_all x4, waiting for transfers between devices, sum_at_owner(): tiles = lax.all_to_all(cut_along(x, dim, count), axis, 0, 0, tiled=True)  149 us
    all_to_all x4, waiting for transfers between devices, combine_tensor(): lax.all_to_all(jnp.stack([share] * lax.axis_size('tensor')), 'tensor', 0, 0)  67.9 us
    all_to_all x3, waiting for transfers between devices, copy_for_each(): lax.all_to_all(jnp.broadcast_to(x[None], (count, *x.shape)), axis, 0, 0,...  25.9 us
    all_to_all x1, starting transfers between devices, mirror_terms(): lax.all_to_all(split[1], 'section', split_axis=1, concat_axis=1, tiled=True)  21.1 us
    all_to_all x4, starting transfers between devices, combine_tensor(): lax.all_to_all(jnp.stack([share] * lax.axis_size('tensor')), 'tensor', 0, 0)  18.9 us
    all_to_all x1, waiting for transfers between devices, mirror_terms(): lax.all_to_all(split[1], 'section', split_axis=1, concat_axis=1, tiled=True)  18.7 us
    all_to_all x2, starting transfers between devices, reflect_blocks(): lax.all_to_all(shortened(flipped), 'section', split_axis=1, concat_axis=1...  18.4 us
    all_to_all x4, starting transfers between devices, sum_at_owner(): tiles = lax.all_to_all(cut_along(x, dim, count), axis, 0, 0, tiled=True)  16.5 us
  transfers between devices with their start and end apart: 19, of which 17 were waited for; matrix products, arithmetic and copies ran while one was open for 13% of the time, Pallas kernels for 0%

profile of v1, /device:TPU:64, one launch (start us, length us, event | category | flops | bytes accessed | tf_op | source)
XLA Modules:
  0.0 487.5 jit_solution(15942455178023011693)
XLA Ops:
  2.3 9.2 %all-to-all-start.3 = ((f32[16,1,224]{2,1,0:T(1,128)}), f32[16,1,224]{2,1,0:T(1,128)S(1)}, u32[]{:S(2)}, u32[]{:S(2)}) async-start(f32[16,1,224]{2,1,0:T(1,128)} %broadcast_in_dim.40), calls=%async_computation.3 | async-start | bytes 32768 | tf_op jit(solution)/shard_map/all_to_all | solution.py:35
  13.7 7.8 %all-to-all-done.3 = f32[16,1,224]{2,1,0:T(1,128)S(1)} async-done(((f32[16,1,224]{2,1,0:T(1,128)}), f32[16,1,224]{2,1,0:T(1,128)S(1)}, u32[]{:S(2)}, u32[]{:S(2)}) %all-to-all-start.3) | async-done | bytes 14368 | tf_op jit(solution)/shard_map/all_to_all | solution.py:35
  26.5 9.1 %all-to-all-done = f32[16,1,224]{2,1,0:T(1,128)S(1)} async-done(((f32[16,1,224]{2,1,0:T(1,128)}), f32[16,1,224]{2,1,0:T(1,128)S(1)}, u32[]{:S(2)}, u32[]{:S(2)}) %all-to-all-start) | async-done | bytes 14368 | tf_op jit(solution)/shard_map/all_to_all | solution.py:35
  35.6 7.3 %all-to-all-start.12 = ((bf16[224,16,32]{0,2,1:T(8,128)(2,1)}), bf16[224,16,32]{0,2,1:T(8,128)(2,1)S(1)}, u32[]{:S(2)}, u32[]{:S(2)}) async-start(bf16[224,16,32]{0,2,1:T(8,128)(2,1)} %multiply_convert_fusion), calls=%async_computation.12 | async-start | bytes 524288 | tf_op jit(solution)/shard_map/all_to_all | solution.py:71
  47.9 4.2 all-to-all-done.12
  52.1 4.4 all-to-all-start.4
  62.1 42.9 %all-to-all-done.4 = f32[16,224,128]{2,1,0:T(8,128)} async-done(((f32[16,224,128]{2,1,0:T(8,128)}), f32[16,224,128]{2,1,0:T(8,128)}, u32[]{:S(2)}, u32[]{:S(2)}) %all-to-all-start.4) | async-done | bytes 1835040 | tf_op jit(solution)/shard_map/all_to_all | solution.py:21
  105.0 3.7 all-to-all-start.1
  110.4 38.4 %all-to-all-done.1 = f32[16,224,128]{2,1,0:T(8,128)S(1)} async-done(((f32[16,224,128]{2,1,0:T(8,128)}), f32[16,224,128]{2,1,0:T(8,128)S(1)}, u32[]{:S(2)}, u32[]{:S(2)}) %all-to-all-start.1) | async-done | bytes 1835040 | tf_op jit(solution)/shard_map/all_to_all | solution.py:21
  149.7 3.6 all-to-all-start.5
  160.3 12.1 %all-to-all-done.5 = bf16[16,224,128]{2,1,0:T(8,128)(2,1)S(1)} async-done(((bf16[16,224,128]{2,1,0:T(8,128)(2,1)}), bf16[16,224,128]{2,1,0:T(8,128)(2,1)S(1)}, u32[]{:S(2)}, u32[]{:S(2)}) %all-to-all-start.5) | async-done | bytes 917536 | tf_op jit(solution)/shard_map/all_to_all | solution.py:51
  172.3 13.3 %all-to-all-start.13 = ((bf16[224,16,32]{0,2,1:T(8,128)(2,1)}), bf16[224,16,32]{0,2,1:T(8,128)(2,1)S(1)}, u32[]{:S(2)}, u32[]{:S(2)}) async-start(bf16[224,16,32]{0,2,1:T(8,128)(2,1)} %rev.8), calls=%async_computation.13 | async-start | bytes 524288 | tf_op jit(solution)/shard_map/all_to_all | solution.py:59
  190.0 4.3 all-to-all-done.13
  195.3 4.0 all-to-all-start.2
  204.9 23.3 %all-to-all-done.2 = bf16[16,224,128]{2,1,0:T(8,128)(2,1)S(1)} async-done(((bf16[16,224,128]{2,1,0:T(8,128)(2,1)}), bf16[16,224,128]{2,1,0:T(8,128)(2,1)S(1)}, u32[]{:S(2)}, u32[]{:S(2)}) %all-to-all-start.2) | async-done | bytes 917536 | tf_op jit(solution)/shard_map/all_to_all | solution.py:51
  229.1 3.9 all-to-all-start.9
  246.0 32.5 %all-to-all-done.9 = f32[16,224,128]{2,1,0:T(8,128)S(1)} async-done(((f32[16,224,128]{2,1,0:T(8,128)}), f32[16,224,128]{2,1,0:T(8,128)S(1)}, u32[]{:S(2)}, u32[]{:S(2)}) %all-to-all-start.9) | async-done | bytes 1835040 | tf_op jit(solution)/shard_map/all_to_all | solution.py:21
  278.5 4.4 all-to-all-start.6
  283.0 34.9 %all-to-all-done.6 = f32[16,224,128]{2,1,0:T(8,128)} async-done(((f32[16,224,128]{2,1,0:T(8,128)}), f32[16,224,128]{2,1,0:T(8,128)}, u32[]{:S(2)}, u32[]{:S(2)}) %all-to-all-start.6) | async-done | bytes 1835040 | tf_op jit(solution)/shard_map/all_to_all | solution.py:21
  319.0 7.6 %all-to-all-start.10 = ((bf16[16,224,128]{2,1,0:T(8,128)(2,1)}), bf16[16,224,128]{2,1,0:T(8,128)(2,1)}, u32[]{:S(2)}, u32[]{:S(2)}) async-start(bf16[16,224,128]{2,1,0:T(8,128)(2,1)} %stack.11), calls=%async_computation.10 | async-start | bytes 1835008 | tf_op jit(solution)/shard_map/all_to_all | solution.py:51
  328.2 17.5 %all-to-all-done.10 = bf16[16,224,128]{2,1,0:T(8,128)(2,1)} async-done(((bf16[16,224,128]{2,1,0:T(8,128)(2,1)}), bf16[16,224,128]{2,1,0:T(8,128)(2,1)}, u32[]{:S(2)}, u32[]{:S(2)}) %all-to-all-start.10) | async-done | bytes 917536 | tf_op jit(solution)/shard_map/all_to_all | solution.py:51
  346.8 3.6 all-to-all-start.7
  354.3 15.2 %all-to-all-done.7 = bf16[16,224,128]{2,1,0:T(8,128)(2,1)S(1)} async-done(((bf16[16,224,128]{2,1,0:T(8,128)(2,1)}), bf16[16,224,128]{2,1,0:T(8,128)(2,1)S(1)}, u32[]{:S(2)}, u32[]{:S(2)}) %all-to-all-start.7) | async-done | bytes 917536 | tf_op jit(solution)/shard_map/all_to_all | solution.py:51
  369.5 13.0 %all_to_all.84 = f32[16,1,224]{2,1,0:T(1,128)S(1)} all-to-all(f32[16,1,224]{2,1,0:T(1,128)S(1)} %broadcast_in_dim.44), channel_id=1, replica_groups=mesh['section'=16,'tensor'=16] {'tensor'}, dimensions={0} | all-to-all | bytes 28672 | tf_op jit(solution)/shard_map/all_to_all | solution.py:35
  382.4 21.1 %all-to-all-start.14 = ((bf16[224,16,128]{2,0,1:T(8,128)(2,1)}), bf16[224,16,128]{2,0,1:T(8,128)(2,1)S(1)}, u32[]{:S(2)}, u32[]{:S(2)}) async-start(bf16[224,16,128]{2,0,1:T(8,128)(2,1)} %bitcast.43), calls=%async_computation.14 | async-start | bytes 1835008 | tf_op jit(solution)/shard_map/all_to_all | solution.py:72
  408.1 18.7 %all-to-all-done.14 = bf16[224,16,128]{2,0,1:T(8,128)(2,1)S(1)} async-done(((bf16[224,16,128]{2,0,1:T(8,128)(2,1)}), bf16[224,16,128]{2,0,1:T(8,128)(2,1)S(1)}, u32[]{:S(2)}, u32[]{:S(2)}) %all-to-all-start.14) | async-done | bytes 917536 | tf_op jit(solution)/shard_map/all_to_all | solution.py:72
  431.9 8.9 %all-to-all-done.8 = f32[16,1,224]{2,1,0:T(1,128)S(1)} async-done(((f32[16,1,224]{2,1,0:T(1,128)}), f32[16,1,224]{2,1,0:T(1,128)S(1)}, u32[]{:S(2)}, u32[]{:S(2)}) %all-to-all-start.8) | async-done | bytes 14368 | tf_op jit(solution)/shard_map/all_to_all | solution.py:35
  440.8 5.1 %all-to-all-start.15 = ((bf16[224,16,128]{2,0,1:T(8,128)(2,1)}), bf16[224,16,128]{2,0,1:T(8,128)(2,1)S(1)}, u32[]{:S(2)}, u32[]{:S(2)}) async-start(bf16[224,16,128]{2,0,1:T(8,128)(2,1)} %rev.9), calls=%async_computation.15 | async-start | bytes 1835008 | tf_op jit(solution)/shard_map/all_to_all | solution.py:59
  454.1 4.6 collective-permute-start.1
  461.5 3.5 collective-permute-start
  467.8 6.8 %collective-permute-done.3 = bf16[224,512]{1,0:T(8,128)(2,1)S(1)} collective-permute-done((bf16[224,512]{1,0:T(8,128)(2,1)}, bf16[224,512]{1,0:T(8,128)(2,1)S(1)}, u32[]{:S(2)}, u32[]{:S(2)}) %collective-permute-start.3) | collective-permute-done | bytes 229408 | tf_op jit(solution)/shard_map/ppermute | solution.py:45
  478.9 4.9 %add_bitcast_fusion = f32[1,512,2048]{2,1,0:T(8,128)} fusion(f32[512,2048]{1,0:T(8,128)} %fusion.34, bf16[224,512]{0,1:T(8,128)(2,1)S(1)} %bitcast.230, bf16[224,16,128]{2,0,1:T(8,128)(2,1)S(1)} %all-to-all-done.15), kind=kOutput, calls=%fused_computation.4 | convolution fusion | flops 470810624 | bytes 9535488 | tf_op jit(solution)/shard_map/dot_general | solution.py:143
  (149 shorter events, 92.3 us)
Async XLA Ops:
  2.3 19.2 %all-to-all-start.3 = ((f32[16,1,224]{2,1,0:T(1,128)}), f32[16,1,224]{2,1,0:T(1,128)S(1)}, u32[]{:S(2)}, u32[]{:S(2)}) async-start(f32[16,1,224]{2,1,0:T(1,128)} %broadcast_in_dim.40), calls=%async_computation.3 | async-start | bytes 32768 | tf_op jit(solution)/shard_map/all_to_all | solution.py:35
  22.2 13.4 %all-to-all-start = ((f32[16,1,224]{2,1,0:T(1,128)}), f32[16,1,224]{2,1,0:T(1,128)S(1)}, u32[]{:S(2)}, u32[]{:S(2)}) async-start(f32[16,1,224]{2,1,0:T(1,128)} %broadcast_in_dim.36), calls=%async_computation | async-start | bytes 32768 | tf_op jit(solution)/shard_map/all_to_all | solution.py:35
  25.7 20.1 %copy-start.26 = (f32[224]{0:T(256)}, f32[224]{0:T(256)S(1)}, u32[]{:S(2)}) copy-start(f32[224]{0:T(256)S(1)} %add_rsqrt_fusion) | copy-start | bytes 2692
  35.6 16.5 %all-to-all-start.12 = ((bf16[224,16,32]{0,2,1:T(8,128)(2,1)}), bf16[224,16,32]{0,2,1:T(8,128)(2,1)S(1)}, u32[]{:S(2)}, u32[]{:S(2)}) async-start(bf16[224,16,32]{0,2,1:T(8,128)(2,1)} %multiply_convert_fusion), calls=%async_computation.12 | async-start | bytes 524288 | tf_op jit(solution)/shard_map/all_to_all | solution.py:71
  52.1 7.4 %copy-start.14 = (bf16[224,16,32]{0,2,1:T(8,128)(2,1)}, bf16[224,16,32]{0,2,1:T(8,128)(2,1)S(1)}, u32[]{:S(2)}) copy-start(bf16[224,16,32]{0,2,1:T(8,128)(2,1)S(1)} %all-to-all-done.12) | copy-start | bytes 688132
  52.1 52.9 %all-to-all-start.4 = ((f32[16,224,128]{2,1,0:T(8,128)}), f32[16,224,128]{2,1,0:T(8,128)}, u32[]{:S(2)}, u32[]{:S(2)}) async-start(f32[16,224,128]{2,1,0:T(8,128)} %convolution_bitcast_fusion), calls=%async_computation.4 | async-start | bytes 3670016 | tf_op jit(solution)/shard_map/all_to_all | solution.py:21
  105.0 43.7 %all-to-all-start.1 = ((f32[16,224,128]{2,1,0:T(8,128)}), f32[16,224,128]{2,1,0:T(8,128)S(1)}, u32[]{:S(2)}, u32[]{:S(2)}) async-start(f32[16,224,128]{2,1,0:T(8,128)} %convolution_bitcast_fusion.1), calls=%async_computation.1 | async-start | bytes 3670016 | tf_op jit(solution)/shard_map/all_to_all | solution.py:21
  149.7 22.6 %all-to-all-start.5 = ((bf16[16,224,128]{2,1,0:T(8,128)(2,1)}), bf16[16,224,128]{2,1,0:T(8,128)(2,1)S(1)}, u32[]{:S(2)}, u32[]{:S(2)}) async-start(bf16[16,224,128]{2,1,0:T(8,128)(2,1)} %stack.9), calls=%async_computation.5 | async-start | bytes 1835008 | tf_op jit(solution)/shard_map/all_to_all | solution.py:51
  172.3 21.9 %all-to-all-start.13 = ((bf16[224,16,32]{0,2,1:T(8,128)(2,1)}), bf16[224,16,32]{0,2,1:T(8,128)(2,1)S(1)}, u32[]{:S(2)}, u32[]{:S(2)}) async-start(bf16[224,16,32]{0,2,1:T(8,128)(2,1)} %rev.8), calls=%async_computation.13 | async-start | bytes 524288 | tf_op jit(solution)/shard_map/all_to_all | solution.py:59
  188.3 7.0 %copy-start.29 = (f32[4,224]{1,0:T(4,128)}, f32[4,224]{1,0:T(4,128)S(1)}, u32[]{:S(2)}) copy-start(f32[4,224]{1,0:T(4,128)S(1)} %get-tuple-element.17) | copy-start | bytes 10756
  188.3 11.0 %copy-start.3 = (bf16[224,4,128]{2,1,0:T(4,128)(2,1)S(1)}, bf16[224,4,128]{2,1,0:T(4,128)(2,1)}, u32[]{:S(2)}) copy-start(bf16[224,4,128]{2,1,0:T(4,128)(2,1)} %reshape.266) | copy-start | bytes 688132
  190.0 11.5 %copy-start.4 = (bf16[224,4,128]{2,1,0:T(4,128)(2,1)}, bf16[224,4,128]{2,1,0:T(4,128)(2,1)S(1)}, u32[]{:S(2)}) copy-start(bf16[224,4,128]{2,1,0:T(4,128)(2,1)S(1)} %convolution_bitcast_fusion.11) | copy-start | bytes 688132
  195.3 32.8 %all-to-all-start.2 = ((bf16[16,224,128]{2,1,0:T(8,128)(2,1)}), bf16[16,224,128]{2,1,0:T(8,128)(2,1)S(1)}, u32[]{:S(2)}, u32[]{:S(2)}) async-start(bf16[16,224,128]{2,1,0:T(8,128)(2,1)} %stack.8), calls=%async_computation.2 | async-start | bytes 1835008 | tf_op jit(solution)/shard_map/all_to_all | solution.py:51
  229.1 49.4 %all-to-all-start.9 = ((f32[16,224,128]{2,1,0:T(8,128)}), f32[16,224,128]{2,1,0:T(8,128)S(1)}, u32[]{:S(2)}, u32[]{:S(2)}) async-start(f32[16,224,128]{2,1,0:T(8,128)} %copy.197), calls=%async_computation.9 | async-start | bytes 3670016 | tf_op jit(solution)/shard_map/all_to_all | solution.py:21
  238.2 3.7 copy-start.15
  278.5 39.4 %all-to-all-start.6 = ((f32[16,224,128]{2,1,0:T(8,128)}), f32[16,224,128]{2,1,0:T(8,128)}, u32[]{:S(2)}, u32[]{:S(2)}) async-start(f32[16,224,128]{2,1,0:T(8,128)} %copy.186), calls=%async_computation.6 | async-start | bytes 3670016 | tf_op jit(solution)/shard_map/all_to_all | solution.py:21
  319.0 26.8 %all-to-all-start.10 = ((bf16[16,224,128]{2,1,0:T(8,128)(2,1)}), bf16[16,224,128]{2,1,0:T(8,128)(2,1)}, u32[]{:S(2)}, u32[]{:S(2)}) async-start(bf16[16,224,128]{2,1,0:T(8,128)(2,1)} %stack.11), calls=%async_computation.10 | async-start | bytes 1835008 | tf_op jit(solution)/shard_map/all_to_all | solution.py:51
  326.6 23.8 %copy-start.8 = (bf16[4,224,224]{1,2,0:T(8,128)(2,1)S(1)}, bf16[4,224,224]{1,2,0:T(8,128)(2,1)}, u32[]{:S(2)}) copy-start(bf16[4,224,224]{1,2,0:T(8,128)(2,1)} %copy-done.7) | copy-start | bytes 1204228
  326.6 23.8 %copy-start.18 = (bf16[224,4,128]{2,1,0:T(4,128)(2,1)S(1)}, bf16[224,4,128]{2,1,0:T(4,128)(2,1)}, u32[]{:S(2)}) copy-start(bf16[224,4,128]{2,1,0:T(4,128)(2,1)} %copy-done.17) | copy-start | bytes 688132
  346.8 22.7 %all-to-all-start.7 = ((bf16[16,224,128]{2,1,0:T(8,128)(2,1)}), bf16[16,224,128]{2,1,0:T(8,128)(2,1)S(1)}, u32[]{:S(2)}, u32[]{:S(2)}) async-start(bf16[16,224,128]{2,1,0:T(8,128)(2,1)} %stack.10), calls=%async_computation.7 | async-start | bytes 1835008 | tf_op jit(solution)/shard_map/all_to_all | solution.py:51
  350.8 52.7 %copy-start.20 = (bf16[224,4,128]{2,1,0:T(4,128)(2,1)S(1)}, bf16[224,4,128]{2,1,0:T(4,128)(2,1)}, u32[]{:S(2)}) copy-start(bf16[224,4,128]{2,1,0:T(4,128)(2,1)} %copy-done.19) | copy-start | bytes 688132
  382.4 44.3 %all-to-all-start.14 = ((bf16[224,16,128]{2,0,1:T(8,128)(2,1)}), bf16[224,16,128]{2,0,1:T(8,128)(2,1)S(1)}, u32[]{:S(2)}, u32[]{:S(2)}) async-start(bf16[224,16,128]{2,0,1:T(8,128)(2,1)} %bitcast.43), calls=%async_computation.14 | async-start | bytes 1835008 | tf_op jit(solution)/shard_map/all_to_all | solution.py:72
  408.1 37.8 %copy-start.5 = (bf16[224,4,128]{2,1,0:T(4,128)(2,1)S(1)}, bf16[224,4,128]{2,1,0:T(4,128)(2,1)}, u32[]{:S(2)}) copy-start(bf16[224,4,128]{2,1,0:T(4,128)(2,1)} %copy-done.4) | copy-start | bytes 688132
  427.4 13.4 %all-to-all-start.8 = ((f32[16,1,224]{2,1,0:T(1,128)}), f32[16,1,224]{2,1,0:T(1,128)S(1)}, u32[]{:S(2)}, u32[]{:S(2)}) async-start(f32[16,1,224]{2,1,0:T(1,128)} %broadcast_in_dim.42), calls=%async_computation.8 | async-start | bytes 32768 | tf_op jit(solution)/shard_map/all_to_all | solution.py:35
  440.8 38.1 %all-to-all-start.15 = ((bf16[224,16,128]{2,0,1:T(8,128)(2,1)}), bf16[224,16,128]{2,0,1:T(8,128)(2,1)S(1)}, u32[]{:S(2)}, u32[]{:S(2)}) async-start(bf16[224,16,128]{2,0,1:T(8,128)(2,1)} %rev.9), calls=%async_computation.15 | async-start | bytes 1835008 | tf_op jit(solution)/shard_map/all_to_all | solution.py:59
  447.1 11.7 %copy-start.16 = (bf16[1,224,512]{2,1,0:T(8,128)(2,1)S(1)}, bf16[1,224,512]{2,1,0:T(8,128)(2,1)}, u32[]{:S(2)}) copy-start(bf16[1,224,512]{2,1,0:T(8,128)(2,1)} %param.8) | copy-start | bytes 688132
  448.4 10.3 %copy-start.21 = (f32[224,512]{1,0:T(8,128)S(1)}, f32[224,512]{1,0:T(8,128)}, u32[]{:S(2)}) copy-start(f32[224,512]{1,0:T(8,128)} %get-tuple-element.16) | copy-start | bytes 1376260
  450.7 23.9 %collective-permute-start.3 = (bf16[224,512]{1,0:T(8,128)(2,1)}, bf16[224,512]{1,0:T(8,128)(2,1)S(1)}, u32[]{:S(2)}, u32[]{:S(2)}) collective-permute-start(bf16[224,512]{1,0:T(8,128)(2,1)} %get-tuple-element.9), channel_id=1, source_target_pairs={{0,16},{16,32},{32,48},{48,64},{64,80},{80,96},{96,112},{112,128},... | collective-permute-start | bytes 688136 | tf_op jit(solution)/shard_map/ppermute | solution.py:45
  454.1 20.6 %collective-permute-start.1 = (bf16[224,512]{1,0:T(8,128)(2,1)}, bf16[224,512]{1,0:T(8,128)(2,1)}, u32[]{:S(2)}, u32[]{:S(2)}) collective-permute-start(bf16[224,512]{1,0:T(8,128)(2,1)} %get-tuple-element.10), channel_id=1, source_target_pairs={{16,0},{32,16},{48,32},{64,48},{80,64},{96,80},{112,96},{128,112},... | collective-permute-start | bytes 688136 | tf_op jit(solution)/shard_map/ppermute | solution.py:45
  459.0 16.6 %collective-permute-start.2 = (bf16[224,512]{1,0:T(8,128)(2,1)S(1)}, bf16[224,512]{1,0:T(8,128)(2,1)S(1)}, u32[]{:S(2)}, u32[]{:S(2)}) collective-permute-start(bf16[224,512]{1,0:T(8,128)(2,1)S(1)} %get-tuple-element.11), channel_id=1, source_target_pairs={{16,0},{32,16},{48,32},{64,48},{80,64},{96,80},{112,96},{128,112},... | collective-permute-start | bytes 688136 | tf_op jit(solution)/shard_map/ppermute | solution.py:45
  461.4 17.4 %copy-start.13 = (bf16[224,16,32]{0,2,1:T(8,128)(2,1)S(1)}, bf16[224,16,32]{0,2,1:T(8,128)(2,1)}, u32[]{:S(2)}) copy-start(bf16[224,16,32]{0,2,1:T(8,128)(2,1)} %copy-done.12) | copy-start | bytes 688132
  461.5 17.4 %collective-permute-start = (bf16[224,512]{1,0:T(8,128)(2,1)S(1)}, bf16[224,512]{1,0:T(8,128)(2,1)S(1)}, u32[]{:S(2)}, u32[]{:S(2)}) collective-permute-start(bf16[224,512]{1,0:T(8,128)(2,1)S(1)} %get-tuple-element.12), channel_id=1, source_target_pairs={{0,16},{16,32},{32,48},{48,64},{64,80},{80,96},{96,112},{112,128},... | collective-permute-start | bytes 688136 | tf_op jit(solution)/shard_map/ppermute | solution.py:45
  (17 other events, 26.4 us)
